TPU v7x, 128 devices: a whole 4x4x4 slice. The times are simulated.
128 devices in a mesh: seq: 16 (over x, y), exp: 8 (over z, core).
Axes of the slice: x: 4, y: 4, z: 4, core: 2. Of those that a mesh axis runs over, the one named last changes fastest.
Arguments:
- upstream: bfloat16 [8192, 6144], P(('seq', 'exp')), may hold values from -6 to 6
- out_weight: bfloat16 [4096, 6144], P('exp'), may hold values from -0.078125 to 0.078125
- queries: bfloat16 [8192, 4096], P('seq', 'exp'), may hold values from -6 to 6
- keys: bfloat16 [8192, 4096], P('seq', 'exp'), may hold values from -6 to 6
- values: bfloat16 [8192, 4096], P('seq', 'exp'), may hold values from -6 to 6
- log_decay: float32 [32, 8192], P('exp', 'seq'), may hold values from -0.8 to 0, as said below
- expert_ids: int32 [8192, 2], P(('seq', 'exp')), may hold values from 0 to 15, all different within a row; in each aligned block of 64 rows (0 to 63, 64 to 127, ...) at most 9 rows name the same one
- gate_probs: float32 [8192, 2], P(('seq', 'exp')), may hold values from 0.05 to 0.95
- activations: bfloat16 [16, 4608, 1152], P('exp', 'seq'), may hold values from -1.5 to 1.5
Outputs:
- d_queries: bfloat16 [8192, 4096], P('seq', 'exp')
- d_keys: bfloat16 [8192, 4096], P('seq', 'exp')
- d_values: bfloat16 [8192, 4096], P('seq', 'exp')
- d_down: bfloat16 [16, 4608, 6144], P('exp', 'seq')
Inputs may be any that keep to these rules, and one draw needn't show every extreme that they name: `expert_ids`: each row names two different experts. In every block of 64 rows no expert is named more than 9 times, and in every draw some block names some expert exactly 9 times. `log_decay`: negative at every position.
All inputs are finite; a program needn't handle non-finite values.
Results may differ from a plain program's by a relative error of at most 0.005.
Values may be sent and summed in bfloat16 or wider, within the bound.
A program may use at most 192 MiB of HBM per device.

v0:
```python
import math
import jax
import jax.numpy as jnp
from jax import lax
from jax.sharding import PartitionSpec as P

HEAD = 128
EXPERTS = 16
HIGH = lax.Precision.HIGHEST


def prefix(value, axis, join, neutral, backward):
    count, mine = (lax.axis_size(axis), lax.axis_index(axis))
    pieces = jax.tree.map(lambda part: lax.all_gather(part, axis), value)
    if backward:
        pieces = jax.tree.map(lambda part: part[::-1], pieces)
        mine = count - 1 - mine
    so_far = jax.tree.map(
        lambda part, zero: jnp.full_like(part, 0) + jnp.asarray(zero, part.dtype), value, neutral
    )

    def hop(position, so_far):
        longer = join(so_far, jax.tree.map(lambda part: part[position], pieces))
        return jax.tree.map(lambda new, old: jnp.where(position < mine, new, old), longer, so_far)

    return lax.fori_loop(0, count - 1, hop, so_far)


def block_terms(
    raw_query,
    raw_key,
    raw_value,
    raw_grad,
    query_heads,
    key_heads,
    value_heads,
    grad_heads,
    cumulative,
    lead,
    tail,
    state_in,
    adjoint_in,
):
    length = cumulative.shape[1]
    position = jnp.arange(length)
    lower = position[:, None] >= position[None, :]
    spread = cumulative[:, :, None] - cumulative[:, None, :]
    weights = jnp.where(lower[None], jnp.exp(jnp.minimum(spread, 0.0)), 0.0)
    mixed = (
        jnp.einsum("thf,shf->hts", raw_grad, raw_value, preferred_element_type=jnp.float32)
        * weights
    )
    paired = (
        jnp.einsum("the,she->hts", raw_query, raw_key, preferred_element_type=jnp.float32) * weights
    )
    d_query = jnp.einsum("hts,she->the", mixed, key_heads, precision=HIGH) + lead * jnp.einsum(
        "thf,hef->the", grad_heads, state_in, precision=HIGH
    )
    d_key = jnp.einsum("hts,the->she", mixed, query_heads, precision=HIGH) + tail * jnp.einsum(
        "shf,hef->she", value_heads, adjoint_in, precision=HIGH
    )
    d_value = jnp.einsum("hts,thf->shf", paired, grad_heads, precision=HIGH) + tail * jnp.einsum(
        "she,hef->shf", key_heads, adjoint_in, precision=HIGH
    )
    return (d_query, d_key, d_value)


def forward_join(earlier, later):
    return (earlier[0] * later[0], later[0][:, None, None] * earlier[1] + later[1])


def reverse_join(earlier, later):
    return (earlier[0] * later[0], later[1] + later[0][:, None, None] * earlier[1])


def shards(
    upstream, out_weight, queries, keys, values, log_decay, expert_ids, gate_probs, activations
):
    seq_count = lax.axis_size("seq")
    exp_count = lax.axis_size("exp")
    rows_here = queries.shape[0]
    heads_here = queries.shape[1] // HEAD
    scale = 1.0 / math.sqrt(HEAD * rows_here * seq_count)
    most = activations.shape[2] // (seq_count * exp_count)
    model_width = upstream.shape[1]
    grad_out = jnp.einsum(
        "td,fd->tf",
        lax.all_gather(upstream, "exp", axis=0, tiled=True),
        out_weight,
        preferred_element_type=jnp.float32,
    ).astype(jnp.bfloat16)
    flat_experts = expert_ids.reshape(-1)
    onehot = (flat_experts[:, None] == jnp.arange(EXPERTS, dtype=jnp.int32)[None, :]).astype(
        jnp.int32
    )
    earlier = jnp.cumsum(onehot, axis=0) - onehot
    rank = jnp.sum(earlier * onehot, axis=1)
    slot = flat_experts * most + rank
    routed = (
        (gate_probs[:, :, None] * upstream[:, None, :].astype(jnp.float32))
        .astype(jnp.bfloat16)
        .reshape(-1, model_width)
    )
    select = (jnp.arange(EXPERTS * most, dtype=jnp.int32)[:, None] == slot[None, :]).astype(
        jnp.bfloat16
    )
    outgoing = (
        jnp.dot(select, routed, preferred_element_type=jnp.float32)
        .astype(jnp.bfloat16)
        .reshape(EXPERTS, most, model_width)
    )
    incoming = lax.all_to_all(outgoing, "exp", split_axis=0, concat_axis=1, tiled=True)

    def split_raw(block):
        return block.reshape(rows_here, heads_here, HEAD)

    raw_query = split_raw(queries)
    raw_key = split_raw(keys)
    raw_value = split_raw(values)
    raw_grad = split_raw(grad_out)
    query_heads = raw_query.astype(jnp.float32)
    key_heads = raw_key.astype(jnp.float32)
    value_heads = raw_value.astype(jnp.float32)
    grad_heads = raw_grad.astype(jnp.float32)
    cumulative = jnp.cumsum(log_decay, axis=1)
    totals = cumulative[:, -1]
    lead = jnp.exp(cumulative).T[:, :, None]
    tail = jnp.exp(cumulative[:, -1:] - cumulative).T[:, :, None]
    kv_sum = jnp.einsum("she,shf->hef", key_heads * tail, value_heads, precision=HIGH)
    qo_sum = jnp.einsum("the,thf->hef", query_heads * lead, grad_heads, precision=HIGH)
    head_decay = jnp.exp(totals)
    identity_pair = (
        jnp.ones((heads_here,), jnp.float32),
        jnp.zeros((heads_here, HEAD, HEAD), jnp.float32),
    )
    state_in = prefix((head_decay, kv_sum), "seq", forward_join, identity_pair, False)[1]
    adjoint_in = prefix((head_decay, qo_sum), "seq", reverse_join, identity_pair, True)[1]
    d_query, d_key, d_value = block_terms(
        raw_query,
        raw_key,
        raw_value,
        raw_grad,
        query_heads,
        key_heads,
        value_heads,
        grad_heads,
        cumulative,
        lead,
        tail,
        state_in,
        adjoint_in,
    )
    width = heads_here * HEAD
    d_queries = (scale * d_query).reshape(rows_here, width).astype(jnp.bfloat16)
    d_keys = (scale * d_key).reshape(rows_here, width).astype(jnp.bfloat16)
    d_values = (scale * d_value).reshape(rows_here, width).astype(jnp.bfloat16)
    gathered = lax.all_gather(incoming, "seq", axis=1, tiled=True)
    d_down = jnp.einsum("ehs,esd->ehd", activations, gathered, preferred_element_type=jnp.float32)
    return (d_queries, d_keys, d_values, d_down.astype(jnp.bfloat16))


def solution(mesh):
    return jax.shard_map(
        shards,
        mesh=mesh,
        in_specs=(
            P(("seq", "exp"), None),
            P("exp", None),
            P("seq", "exp"),
            P("seq", "exp"),
            P("seq", "exp"),
            P("exp", "seq"),
            P(("seq", "exp"), None),
            P(("seq", "exp"), None),
            P("exp", "seq", None),
        ),
        out_specs=(P("seq", "exp"), P("seq", "exp"), P("seq", "exp"), P("exp", "seq", None)),
        check_vma=False,
    )
```

profile of v0, /device:TPU:1, one launch (start us, length us, event | category | flops | bytes accessed | tf_op | source)
XLA Modules:
  0.0 360.2 jit_solution(13961593589067682039)
XLA Ops:
  8.0 0.7 reshape.111
  8.7 1.2 reduce-window.6
  10.5 1.3 copy.50
  11.8 2.5 fusion.47
  14.5 1.3 copy.54
  15.7 38.8 %all-gather.8.cloned.1.call-done = bf16[512,6144]{1,0:T(8,128)(2,1)} async-done(((bf16[64,6144]{1,0:T(8,128)(2,1)}), bf16[512,6144]{1,0:T(8,128)(2,1)}) %all-gather.8.cloned.1.call-update) | async-done | bytes 6291472 | tf_op jit(solution)/shard_map/all_gather | solution.py:88
  54.5 8.0 %convolution_convert_fusion.2 = bf16[512,512]{0,1:T(8,128)(2,1)S(1)} fusion(bf16[512,6144]{1,0:T(8,128)(2,1)} %all-gather.8.cloned.1.call-done, bf16[512,6144]{1,0:T(8,128)(2,1)} %param.14), kind=kOutput, calls=%fused_computation.44 | convolution fusion | flops 3221487616 | bytes 13107200 | tf_op jit(solution)/shard_map/td,fd->tf/dot_general | solution.py:86
  62.6 0.8 copy-done.5
  63.4 1.4 fusion.44
  65.1 3.2 mul.145
  68.3 5.1 %mul.146 = f32[128,6144]{1,0:T(8,128)} reshape(f32[64,2,6144]{2,1,0:T(2,128)} %mul.145) | data formatting | bytes 6291456 | tf_op jit(solution)/shard_map/mul | solution.py:100
  74.1 2.6 convolution_convert_fusion.1
  76.7 2.1 reshape.116
  78.8 41.6 %all_to_all.18 = bf16[16,9,6144]{2,1,0:T(8,128)(2,1)S(1)} all-to-all(bf16[16,9,6144]{2,1,0:T(8,128)(2,1)} %reshape.116), channel_id=1, replica_groups=mesh['seq'=16,'exp'=8] {'exp'}, dimensions={0} | all-to-all | bytes 3538944 | tf_op jit(solution)/shard_map/all_to_all | solution.py:112
  120.4 1.9 copy.63
  122.4 1.8 copy.64
  125.8 33.6 %all-reduce = f32[64]{0:T(128)S(1)} all-reduce(f32[64]{0:T(128)S(1)} %bitcast_dynamic-update-slice_fusion), channel_id=2, replica_groups=mesh['seq'=16,'exp'=8] {'seq'}, use_global_device_ids=true, to_apply=%add | all-reduce | flops 64 | bytes 512
  159.5 0.8 iota_compare_fusion
  160.3 2.7 fusion.64
  163.0 16.6 %while.28 = (s32[]{:T(128)}, f32[4,128,128]{2,1,0:T(8,128)S(1)}, s32[]{:T(128)}, f32[16,4]{1,0:T(8,128)S(1)}, f32[16,4,128,128]{3,2,1,0:T(8,128)}, /*index=5*/s32[]{:T(128)}, s32[]{:T(128)}) while((s32[]{:T(128)}, f32[4,128,128]{2,1,0:T(8,128)S(1)}, s32[]{:T(128)}, f32[16,4]{1,0:T(8,128)S(1)}, f32[16,4,128,128]{3,2,1,0:T(8,128)}, ...), condition=%wide.region_3.4_spmd.clone, body=%wide.region_2.3_spmd.clone.sunk | while | flops 262148 | bytes 786585 | solution.py:26
  163.0 1.0 fusion.86
  164.1 1.1 fusion.86
  165.2 1.1 fusion.86
  166.3 1.1 fusion.86
  167.4 1.1 fusion.86
  168.5 1.1 fusion.86
  169.6 1.1 fusion.86
  170.7 1.1 fusion.86
  171.8 1.1 fusion.86
  172.9 1.1 fusion.86
  174.1 1.1 fusion.86
  175.2 1.1 fusion.86
  176.3 1.1 fusion.86
  177.4 1.1 fusion.86
  178.5 1.1 fusion.86
  179.6 1.8 fusion.52
  181.5 3.5 fusion.23
  184.9 1.4 fusion.41
  186.3 2.1 copy.65
  188.5 6.1 %fusion.29 = f32[512,4,128]{0,2,1:T(8,128)} fusion(bf16[512,4,128]{0,2,1:T(8,128)(2,1)S(1)} %bitcast.133, f32[4,512,512]{2,1,0:T(8,128)} %fusion.64, f32[4,512]{1,0:T(4,128)S(1)} %bitcast.141, pred[512,512]{1,0:T(8,128)(4,1)} %iota_compare_fusion), kind=kOutput, calls=%fused_computation.31 | convolution fusion | flops 1614807040 | bytes 6037504 | tf_op jit(solution)/shard_map/hts,thf->shf/dot_general | solution.py:62
  194.6 3.9 %fusion.26 = f32[512,4,128]{0,2,1:T(8,128)} fusion(bf16[512,4,128]{0,2,1:T(8,128)(2,1)S(1)} %bitcast.125, f32[4,512,512]{2,1,0:T(8,128)S(1)} %copy-done.8, f32[4,512]{1,0:T(4,128)S(1)} %bitcast.142, pred[512,512]{1,0:T(8,128)(4,1)S(1)} %copy-done.12), kind=kOutput, calls=%fused_computation.30 | convolution fusion | flops 1614807040 | bytes 6037504 | tf_op jit(solution)/shard_map/hts,the->she/dot_general | solution.py:59
  198.5 4.7 %rev.6 = f32[16,4,128,128]{3,2,1,0:T(8,128)} reverse(f32[16,4,128,128]{3,2,1,0:T(8,128)} %bitcast.134), dimensions={0} | reverse | bytes 8388608 | tf_op jit(solution)/shard_map/rev | solution.py:16
  203.2 16.8 %while.29 = (s32[]{:T(128)}, f32[4,128,128]{2,1,0:T(8,128)S(1)}, s32[]{:T(128)}, f32[16,4,128,128]{3,2,1,0:T(8,128)}, f32[16,4]{1,0:T(8,128)S(1)}, /*index=5*/s32[]{:T(128)}, s32[]{:T(128)}) while((s32[]{:T(128)}, f32[4,128,128]{2,1,0:T(8,128)S(1)}, s32[]{:T(128)}, f32[16,4,128,128]{3,2,1,0:T(8,128)}, f32[16,4]{1,0:T(8,128)S(1)}, ...), condition=%wide.region_5.6_spmd.clone, body=%wide.region_4.5_spmd.clone.sunk | while | flops 262148 | bytes 786585 | solution.py:26
  203.2 1.1 fusion.87
  204.4 1.1 fusion.87
  205.5 1.1 fusion.87
  206.6 1.1 fusion.87
  207.7 1.1 fusion.87
  208.8 1.1 fusion.87
  209.8 1.1 fusion.87
  210.9 1.1 fusion.87
  212.0 1.1 fusion.87
  213.1 1.1 fusion.87
  214.2 1.1 fusion.87
  215.3 1.1 fusion.87
  216.5 1.1 fusion.87
  217.7 1.1 fusion.87
  218.8 1.1 fusion.87
  220.0 1.9 fusion.43
  221.9 1.0 copy.67
  222.9 1.8 fusion.42
  224.7 1.0 copy.66
  225.7 107.3 %all-gather.10.cloned.1.call-done = bf16[2,1152,6144]{2,1,0:T(8,128)(2,1)} async-done(((bf16[2,72,6144]{2,1,0:T(8,128)(2,1)}), bf16[2,1152,6144]{2,1,0:T(8,128)(2,1)}) %all-gather.10.cloned.1.call-update) | async-done | bytes 28311568 | tf_op jit(solution)/shard_map/all_gather | solution.py:157
  333.0 20.7 %fusion.2 = bf16[2,288,6144]{2,1,0:T(8,128)(2,1)} fusion(bf16[2,288,1152]{2,1,0:T(8,128)(2,1)S(1)} %copy-done, bf16[2,1152,6144]{2,1,0:T(8,128)(2,1)} %all-gather.10.cloned.1.call-done), kind=kOutput, calls=%fused_computation.7 | convolution fusion | flops 8157265920 | bytes 36716544 | tf_op jit(solution)/shard_map/ehs,esd->ehd/dot_general | solution.py:158
  (93 shorter events, 3.9 us)
Async XLA Ops:
  7.2 325.9 %copy-start = (bf16[2,288,1152]{2,1,0:T(8,128)(2,1)S(1)}, bf16[2,288,1152]{2,1,0:T(8,128)(2,1)}, u32[]{:S(2)}) copy-start(bf16[2,288,1152]{2,1,0:T(8,128)(2,1)} %param.21) | copy-start | bytes 3981316
  7.2 47.4 %all-gather.8.cloned.1.call-start = ((), (), s32[]{:S(2)}) async-start(), calls=%async_computation.1 | async-start | bytes 7077888 | tf_op jit(solution)/shard_map/all_gather | solution.py:88
  7.9 155.1 %all-gather.12.cloned.1.call-start = ((), (), s32[]{:S(2)}) async-start(), calls=%async_computation.3 | async-start | bytes 4456448 | tf_op jit(solution)/shard_map/all_gather | solution.py:14
  11.7 2.7 copy-start.3
  14.4 184.1 %all-gather.14.cloned.1.call-start = ((), (), s32[]{:S(2)}) async-start(), calls=%async_computation.4 | async-start | bytes 4456448 | tf_op jit(solution)/shard_map/all_gather | solution.py:14
  15.7 46.9 %copy-start.1 = (bf16[512,512]{0,1:T(8,128)(2,1)}, bf16[512,512]{0,1:T(8,128)(2,1)S(1)}, u32[]{:S(2)}) copy-start(bf16[512,512]{0,1:T(8,128)(2,1)S(1)} %copy.54) | copy-start | bytes 1572868
  15.7 49.1 %copy-start.13 = (s32[64,2]{0,1:T(2,128)S(1)}, s32[64,2]{0,1:T(2,128)}, u32[]{:S(2)}) copy-start(s32[64,2]{0,1:T(2,128)} %param.19) | copy-start | bytes 1540
  15.7 49.3 %copy-start.9 = (bf16[64,6144]{1,0:T(8,128)(2,1)S(1)}, bf16[64,6144]{1,0:T(8,128)(2,1)}, u32[]{:S(2)}) copy-start(bf16[64,6144]{1,0:T(8,128)(2,1)} %param.13) | copy-start | bytes 2359300
  62.6 0.8 copy-start.5
  64.8 268.3 %all-gather.10.cloned.1.call-start = ((), (), s32[]{:S(2)}) async-start(), calls=%async_computation.2 | async-start | bytes 30081024 | tf_op jit(solution)/shard_map/all_gather | solution.py:157
  65.1 8.3 %copy-start.14 = (f32[64,2]{0,1:T(2,128)S(1)}, f32[64,2]{0,1:T(2,128)}, u32[]{:S(2)}) copy-start(f32[64,2]{0,1:T(2,128)} %param.20) | copy-start | bytes 1540
  120.4 3.8 %copy-start.15 = (u32[128]{0:T(128)S(1)}, u32[128]{0:T(128)}, u32[]{:S(2)}) copy-start(u32[128]{0:T(128)} %constant.76) | copy-start | bytes 1540
  120.4 39.9 %copy-start.2 = (bf16[512,512]{0,1:T(8,128)(2,1)S(1)}, bf16[512,512]{0,1:T(8,128)(2,1)}, u32[]{:S(2)}) copy-start(bf16[512,512]{0,1:T(8,128)(2,1)} %copy-done.1) | copy-start | bytes 1572868
  120.4 39.9 %copy-start.4 = (bf16[512,512]{0,1:T(8,128)(2,1)S(1)}, bf16[512,512]{0,1:T(8,128)(2,1)}, u32[]{:S(2)}) copy-start(bf16[512,512]{0,1:T(8,128)(2,1)} %copy-done.3) | copy-start | bytes 1572868
  160.3 19.3 %copy-start.6 = (bf16[512,512]{0,1:T(8,128)(2,1)S(1)}, bf16[512,512]{0,1:T(8,128)(2,1)}, u32[]{:S(2)}) copy-start(bf16[512,512]{0,1:T(8,128)(2,1)} %copy-done.5) | copy-start | bytes 1572868
  179.6 1.9 copy-start.11
  181.5 4.9 %copy-start.7 = (f32[4,512,512]{2,1,0:T(8,128)}, f32[4,512,512]{2,1,0:T(8,128)S(1)}, u32[]{:S(2)}) copy-start(f32[4,512,512]{2,1,0:T(8,128)S(1)} %fusion.52) | copy-start | bytes 12582916
  186.3 8.3 %copy-start.12 = (pred[512,512]{1,0:T(8,128)(4,1)S(1)}, pred[512,512]{1,0:T(8,128)(4,1)}, u32[]{:S(2)}) copy-start(pred[512,512]{1,0:T(8,128)(4,1)} %iota_compare_fusion) | copy-start | bytes 786436
  188.5 6.1 %copy-start.8 = (f32[4,512,512]{2,1,0:T(8,128)S(1)}, f32[4,512,512]{2,1,0:T(8,128)}, u32[]{:S(2)}) copy-start(f32[4,512,512]{2,1,0:T(8,128)} %copy-done.7) | copy-start | bytes 12582916
  203.2 19.7 %copy-start.10 = (bf16[512,512]{1,0:T(8,128)(2,1)S(1)}, bf16[512,512]{1,0:T(8,128)(2,1)}, u32[]{:S(2)}) copy-start(bf16[512,512]{1,0:T(8,128)(2,1)} %param.17) | copy-start | bytes 1572868
Sparse Core Ops, SparseCore 0:
  9.7 44.7 all-gather.7
  56.7 50.9 all-gather.11
  109.8 51.4 all-gather.13
  163.3 169.6 all-gather.9
where the time goes:
time: 362 us; the launch traced here: 360 us
  waiting for transfers between devices  147 us (41%)
  blocking collectives  75.2 us (21%)
  matrix products  58.3 us (16%)
  other arithmetic  34.9 us (10%)
  local copies, waits for them, and re-layouts  29.2 us (8%)
  between operations  14.7 us (4%)
    all_gather x1, waiting for transfers between devices, shards(): gathered = lax.all_gather(incoming, 'seq', axis=1, tiled=True)  107 us
    all_to_all x1, blocking collectives, shards(): lax.all_to_all(outgoing, 'exp', split_axis=0, concat_axis=1, tiled=True)  41.6 us
    all_gather x1, waiting for transfers between devices, shards(): lax.all_gather(upstream, 'exp', axis=0, tiled=True)  38.8 us
    unnamed x1, blocking collectives  33.6 us
    select_n x30, other arithmetic, hop(): jnp.where(position < mine, new, old)  32.1 us
    dot_general x1, matrix products, shards(): jnp.einsum('ehs,esd->ehd', activations, gathered, preferred_element_type=...  20.7 us
    unnamed x44, local copies, waits for them, and re-layouts  8.72 us
    mul x3, local copies, waits for them, and re-layouts, shards(): gate_probs[:, :, None] * upstream[:, None, :].astype(jnp.float32)  8.43 us
  transfers between devices with their start and end apart: 4, of which 2 were waited for; matrix products, arithmetic and copies ran while one was open for 28% of the time, Pallas kernels for 0%

commit v1 on v0

--- a/solution.py
+++ b/solution.py
@@ -154,7 +154,9 @@
     d_queries = (scale * d_query).reshape(rows_here, width).astype(jnp.bfloat16)
     d_keys = (scale * d_key).reshape(rows_here, width).astype(jnp.bfloat16)
     d_values = (scale * d_value).reshape(rows_here, width).astype(jnp.bfloat16)
-    gathered = lax.all_gather(incoming, "seq", axis=1, tiled=True)
+    gathered = jnp.concatenate(
+        lax.all_to_all(jnp.stack([incoming] * lax.axis_size("seq")), "seq", 0, 0), axis=1
+    )
     d_down = jnp.einsum("ehs,esd->ehd", activations, gathered, preferred_element_type=jnp.float32)
     return (d_queries, d_keys, d_values, d_down.astype(jnp.bfloat16))
 

time: 362 us -> 779 us (2.15)
  blocking collectives: 75.2 us -> 598 us
  waiting for transfers between devices: 147 us -> 0.74 us
  local copies, waits for them, and re-layouts: 29.2 us -> 55.8 us
    unnamed x1, blocking collectives: 33.6 us -> 536 us
    all_gather x1 -> x0, waiting for transfers between devices: 107 us -> none  [shards(): gathered = lax.all_gather(incoming, 'seq', axis=1, tiled=True)]
    all_gather x1, waiting for transfers between devices: 38.8 us -> 0.02 us  [shards(): lax.all_gather(upstream, 'exp', axis=0, tiled=True)]
    all_to_all x1, blocking collectives: 41.6 us -> 62.3 us  [shards(): lax.all_to_all(outgoing, 'exp', split_axis=0, concat_axis=1, tiled=True)]
    reshape x1 -> x2, local copies, waits for them, and re-layouts: 0.71 us -> 19.7 us  [the longest x1 19.7 us: shards(): jnp.concatenate(lax.all_to_all(jnp.stack([incoming] * lax.axis_size('seq'...]
    another operation x0 -> x2, local copies, waits for them, and re-layouts: none -> 10.1 us  [shards(): jnp.stack([incoming] * lax.axis_size('seq'))]
  transfers between devices with their start and end apart: 4 -> 4, of which waited for: 2 -> 0; matrix products, arithmetic and copies ran while one was open for 28% -> 14% of each run, Pallas kernels for 0% -> 0%
where the time goes in v1:
time: 779 us; the launch traced here: 769 us
  blocking collectives  598 us (77%)
  matrix products  57.3 us (7%)
  local copies, waits for them, and re-layouts  55.8 us (7%)
  other arithmetic  34.5 us (4%)
  between operations  14.7 us (2%)
    unnamed x1, blocking collectives  536 us
    all_to_all x1, blocking collectives, shards(): lax.all_to_all(outgoing, 'exp', split_axis=0, concat_axis=1, tiled=True)  62.3 us
    select_n x30, other arithmetic, hop(): jnp.where(position < mine, new, old)  31.7 us
    dot_general x1, matrix products, shards(): jnp.einsum('ehs,esd->ehd', activations, gathered, preferred_element_type=...  20.9 us
    reshape x1, local copies, waits for them, and re-layouts, shards(): jnp.concatenate(lax.all_to_all(jnp.stack([incoming] * lax.axis_size('seq'...  19.7 us
  transfers between devices with their start and end apart: 4, of which 0 were waited for; matrix products, arithmetic and copies ran while one was open for 14% of the time, Pallas kernels for 0%

profile of v1, /device:TPU:1, one launch (start us, length us, event | category | flops | bytes accessed | tf_op | source)
XLA Modules:
  0.0 769.5 jit_solution(17392569603945511714)
XLA Ops:
  7.2 0.7 all-gather.7.cloned.1.call-update
  7.9 0.8 copy.60
  8.8 0.8 copy.61
  9.7 4.3 mul.145
  14.1 5.1 mul.146
  19.6 2.6 convolution_convert_fusion.1
  22.2 2.1 reshape.125
  24.3 62.3 %all_to_all.20 = bf16[16,9,6144]{2,1,0:T(8,128)(2,1)S(1)} all-to-all(bf16[16,9,6144]{2,1,0:T(8,128)(2,1)} %reshape.125), channel_id=1, replica_groups=mesh['seq'=16,'exp'=8] {'exp'}, dimensions={0} | all-to-all | bytes 3538944 | tf_op jit(solution)/shard_map/all_to_all | solution.py:112
  86.6 1.9 copy.62
  89.0 9.6 %stack.5 = bf16[16,2,72,6144]{3,2,1,0:T(8,128)(2,1)} broadcast(bf16[2,72,6144]{2,1,0:T(8,128)(2,1)S(1)} %copy.63), dimensions={1,2,3} | broadcast | bytes 30081024 | tf_op jit(solution)/shard_map/stack | solution.py:158
  98.6 6.8 all-to-all-start.1
  105.5 1.2 reduce-window.6
  107.6 1.4 fusion.47
  109.5 0.6 dynamic-slice
  110.8 8.0 %convolution_convert_fusion.2 = bf16[512,512]{0,1:T(8,128)(2,1)S(1)} fusion(bf16[512,6144]{1,0:T(8,128)(2,1)} %all-gather.7.cloned.1.call-done, bf16[512,6144]{1,0:T(8,128)(2,1)} %param.14), kind=kOutput, calls=%fused_computation.44 | convolution fusion | flops 3221487616 | bytes 13107200 | tf_op jit(solution)/shard_map/td,fd->tf/dot_general | solution.py:86
  118.8 1.4 fusion.44
  120.3 536.1 %all-reduce = f32[64]{0:T(128)S(1)} all-reduce(f32[64]{0:T(128)S(1)} %bitcast_dynamic-update-slice_fusion), channel_id=2, replica_groups=mesh['seq'=16,'exp'=8] {'seq'}, use_global_device_ids=true, to_apply=%add | all-reduce | flops 64 | bytes 512
  656.6 0.8 iota_compare_fusion
  657.4 2.7 fusion.64
  660.1 16.5 %while.28 = (s32[]{:T(128)}, f32[4,128,128]{2,1,0:T(8,128)S(1)}, s32[]{:T(128)}, f32[16,4]{1,0:T(8,128)S(1)}, f32[16,4,128,128]{3,2,1,0:T(8,128)}, /*index=5*/s32[]{:T(128)}, s32[]{:T(128)}) while((s32[]{:T(128)}, f32[4,128,128]{2,1,0:T(8,128)S(1)}, s32[]{:T(128)}, f32[16,4]{1,0:T(8,128)S(1)}, f32[16,4,128,128]{3,2,1,0:T(8,128)}, ...), condition=%wide.region_3.4_spmd.clone, body=%wide.region_2.3_spmd.clone.sunk | while | flops 262148 | bytes 786593 | solution.py:26
  660.1 1.1 fusion.86
  661.2 1.1 fusion.86
  662.3 1.1 fusion.86
  663.4 1.1 fusion.86
  664.5 1.1 fusion.86
  665.6 1.1 fusion.86
  666.7 1.1 fusion.86
  667.8 1.1 fusion.86
  668.9 1.1 fusion.86
  670.1 1.1 fusion.86
  671.2 1.1 fusion.86
  672.3 1.1 fusion.86
  673.4 1.1 fusion.86
  674.5 1.1 fusion.86
  675.6 1.1 fusion.86
  676.6 1.8 fusion.52
  678.5 3.5 fusion.23
  682.0 1.4 fusion.41
  683.4 2.1 copy.65
  685.5 6.0 fusion.29
  691.5 3.8 fusion.26
  695.3 4.8 rev.6
  700.1 16.5 %while.29 = (s32[]{:T(128)}, f32[4,128,128]{2,1,0:T(8,128)S(1)}, s32[]{:T(128)}, f32[16,4,128,128]{3,2,1,0:T(8,128)}, f32[16,4]{1,0:T(8,128)S(1)}, /*index=5*/s32[]{:T(128)}, s32[]{:T(128)}) while((s32[]{:T(128)}, f32[4,128,128]{2,1,0:T(8,128)S(1)}, s32[]{:T(128)}, f32[16,4,128,128]{3,2,1,0:T(8,128)}, f32[16,4]{1,0:T(8,128)S(1)}, ...), condition=%wide.region_5.6_spmd.clone, body=%wide.region_4.5_spmd.clone.sunk | while | flops 262148 | bytes 786593 | solution.py:26
  700.1 1.0 fusion.87
  701.2 1.1 fusion.87
  702.3 1.1 fusion.87
  703.4 1.1 fusion.87
  704.5 1.1 fusion.87
  705.6 1.1 fusion.87
  706.7 1.1 fusion.87
  707.8 1.1 fusion.87
  708.9 1.1 fusion.87
  710.0 1.1 fusion.87
  711.1 1.1 fusion.87
  712.2 1.1 fusion.87
  713.3 1.1 fusion.87
  714.4 1.1 fusion.87
  715.5 1.1 fusion.87
  716.6 1.8 fusion.42
  718.4 1.0 copy.66
  719.4 1.9 fusion.43
  721.3 1.0 copy.67
  722.3 19.7 %copy.64 = bf16[2,16,72,6144]{3,2,1,0:T(8,128)(2,1)} copy(bf16[2,16,72,6144]{3,2,0,1:T(8,128)(2,1)} %bitcast.22) | data formatting | bytes 56623104 | tf_op jit(solution)/shard_map/reshape | solution.py:157
  742.0 20.9 %fusion.2 = bf16[2,288,6144]{2,1,0:T(8,128)(2,1)} fusion(bf16[2,288,1152]{2,1,0:T(8,128)(2,1)S(1)} %copy-done, bf16[2,1152,6144]{2,1,0:T(8,128)(2,1)} %bitcast.123), kind=kOutput, calls=%fused_computation.7 | convolution fusion | flops 8157265920 | bytes 36716544 | tf_op jit(solution)/shard_map/ehs,esd->ehd/dot_general | solution.py:160
  (84 shorter events, 3.3 us)
Async XLA Ops:
  7.2 734.8 %copy-start = (bf16[2,288,1152]{2,1,0:T(8,128)(2,1)S(1)}, bf16[2,288,1152]{2,1,0:T(8,128)(2,1)}, u32[]{:S(2)}) copy-start(bf16[2,288,1152]{2,1,0:T(8,128)(2,1)} %param.21) | copy-start | bytes 3981316
  7.2 103.6 %all-gather.7.cloned.1.call-start = ((), (), s32[]{:S(2)}) async-start(), calls=%async_computation.2 | async-start | bytes 7077888 | tf_op jit(solution)/shard_map/all_gather | solution.py:88
  98.6 6.9 copy-start.9
  98.6 8.7 %copy-start.5 = (bf16[512,512]{1,0:T(8,128)(2,1)S(1)}, bf16[512,512]{1,0:T(8,128)(2,1)}, u32[]{:S(2)}) copy-start(bf16[512,512]{1,0:T(8,128)(2,1)} %param.16) | copy-start | bytes 1572868
  98.6 9.0 %copy-start.3 = (bf16[512,512]{1,0:T(8,128)(2,1)S(1)}, bf16[512,512]{1,0:T(8,128)(2,1)}, u32[]{:S(2)}) copy-start(bf16[512,512]{1,0:T(8,128)(2,1)} %param.17) | copy-start | bytes 1572868
  98.6 10.7 %copy-start.6 = (bf16[512,512]{1,0:T(8,128)(2,1)S(1)}, bf16[512,512]{1,0:T(8,128)(2,1)}, u32[]{:S(2)}) copy-start(bf16[512,512]{1,0:T(8,128)(2,1)} %param.15) | copy-start | bytes 1572868
  98.6 10.9 %copy-start.10 = (u32[128]{0:T(128)S(1)}, u32[128]{0:T(128)}, u32[]{:S(2)}) copy-start(u32[128]{0:T(128)} %constant.76) | copy-start | bytes 1540
  98.6 623.7 %all-to-all-start.1 = ((bf16[16,2,72,6144]{3,2,1,0:T(8,128)(2,1)}), bf16[16,2,72,6144]{3,2,1,0:T(8,128)(2,1)}, u32[]{:S(2)}, u32[]{:S(2)}) async-start(bf16[16,2,72,6144]{3,2,1,0:T(8,128)(2,1)} %stack.5), calls=%async_computation.1 | async-start | bytes 56623104 | tf_op jit(solution)/shard_map/all_to_all | solution.py:158
  105.4 554.7 %all-gather.9.cloned.1.call-start = ((), (), s32[]{:S(2)}) async-start(), calls=%async_computation.3 | async-start | bytes 4456448 | tf_op jit(solution)/shard_map/all_gather | solution.py:14
  109.0 586.3 %all-gather.11.cloned.1.call-start = ((), (), s32[]{:S(2)}) async-start(), calls=%async_computation.4 | async-start | bytes 4456448 | tf_op jit(solution)/shard_map/all_gather | solution.py:14
  676.6 1.9 copy-start.7
  678.5 4.9 copy-start.1
  683.4 8.1 %copy-start.8 = (pred[512,512]{1,0:T(8,128)(4,1)S(1)}, pred[512,512]{1,0:T(8,128)(4,1)}, u32[]{:S(2)}) copy-start(pred[512,512]{1,0:T(8,128)(4,1)} %iota_compare_fusion) | copy-start | bytes 786436
  685.5 6.1 copy-start.2
  695.3 21.3 %copy-start.4 = (bf16[512,512]{1,0:T(8,128)(2,1)S(1)}, bf16[512,512]{1,0:T(8,128)(2,1)}, u32[]{:S(2)}) copy-start(bf16[512,512]{1,0:T(8,128)(2,1)} %param.17) | copy-start | bytes 1572868
Sparse Core Ops, SparseCore 0:
  9.7 77.4 all-gather.6
  109.1 459.1 all-gather.8
  570.5 105.1 all-gather.10
